TPU v7x, 128 devices: a whole 4x4x4 slice. The times are simulated.
128 devices in a mesh: blk: 16 (over z, x_hi, core), narrow: 8 (over x_lo, y).
Axes of the slice: x: 4 (x_hi: 2, x_lo: 2; x = x_hi * 2 + x_lo), y: 4, z: 4, core: 2. Of those that a mesh axis runs over, the one named last changes fastest.
Arguments:
- student_img: bfloat16 [16384, 1152], P(('blk', 'narrow')), may hold values from -6 to 6
- student_txt: bfloat16 [16384, 1152], P(('blk', 'narrow')), may hold values from -6 to 6
- teacher_img: bfloat16 [16384, 1536], P(('blk', 'narrow')), may hold values from -6 to 6
- teacher_txt: bfloat16 [16384, 1536], P(('blk', 'narrow')), may hold values from -6 to 6
Outputs:
- image_grad: float32 [16384, 1152], P(('blk', 'narrow'))
- text_grad: float32 [16384, 1152], P(('blk', 'narrow'))
All inputs are finite; a program needn't handle non-finite values.
Results may differ from a plain program's by a relative error of at most 0.0097.
Values may be sent and summed in bfloat16 or wider, within the bound.
A program may use at most 128 MiB of HBM per device.

v0:
```python
import jax
import jax.numpy as jnp
from jax import lax
from jax.sharding import PartitionSpec as P

epsilon = 1e-06
logit_scale = 100.0
logit_bias = -4.0


def shifted(x, axis, by):
    count = lax.axis_size(axis)
    return lax.ppermute(x, axis, [(i, (i + by) % count) for i in range(count)])


def unit_rows(raw_rows):
    raw_float = raw_rows.astype(jnp.float32)
    radius = jnp.sqrt(jnp.sum(raw_float * raw_float, axis=1, keepdims=True) + epsilon)
    return (raw_float / radius, radius)


def unit_back(grad_unit, unit_float, radius):
    along_unit = jnp.sum(unit_float * grad_unit, axis=1, keepdims=True)
    return (grad_unit - unit_float * along_unit) / radius


def body(student_img, student_txt, teacher_img, teacher_txt):
    block_count = lax.axis_size("blk")
    block_index = lax.axis_index("blk")
    group_index = lax.axis_index("narrow")
    own_rows = student_txt.shape[0]
    embed_width = student_txt.shape[1]
    image_block, teacher_block = (
        lax.all_gather(student_img, "narrow", axis=0, tiled=True),
        lax.all_gather(teacher_img, "narrow", axis=0, tiled=True),
    )
    block_rows = image_block.shape[0]
    img_float, img_radius = unit_rows(image_block)
    img_unit = img_float.astype(jnp.bfloat16)
    t_img_unit = unit_rows(teacher_block)[0].astype(jnp.bfloat16)
    txt_float, txt_radius = unit_rows(student_txt)
    txt_unit = txt_float.astype(jnp.bfloat16)
    t_txt_unit = unit_rows(teacher_txt)[0].astype(jnp.bfloat16)
    teacher_tile = (
        logit_scale
        * jnp.einsum(
            "rd,cd->rc",
            t_img_unit,
            lax.all_gather(t_txt_unit, "blk", axis=0, tiled=True),
            preferred_element_type=jnp.float32,
        )
        + logit_bias
    )
    row_ids = lax.broadcasted_iota(jnp.int32, (block_rows, own_rows), 0)
    col_ids = lax.broadcasted_iota(jnp.int32, (block_rows, own_rows), 1) + group_index * own_rows
    same_slot = row_ids == col_ids
    pair_start = jnp.zeros((1, 1), jnp.bfloat16)

    def advance(cycle_step, cycle_state):
        text_cur, teach_cur, grad_acc, img_acc, pair_store = cycle_state
        source = (block_index - cycle_step) % block_count
        teacher_logit = lax.dynamic_slice_in_dim(teacher_tile, source * own_rows, own_rows, 1)
        student_logit = (
            logit_scale
            * jnp.einsum("rd,cd->rc", img_unit, text_cur, preferred_element_type=jnp.float32)
            + logit_bias
        )
        positive = jnp.where(same_slot & (source == block_index), 1.0, 0.0).astype(jnp.float32)
        pair_grad = (
            2.0 * jax.nn.sigmoid(student_logit) - jax.nn.sigmoid(teacher_logit) - positive
        ).astype(jnp.bfloat16)
        img_acc = img_acc + jnp.dot(pair_grad, text_cur, preferred_element_type=jnp.float32)
        grad_acc = grad_acc + jnp.einsum(
            "rc,rd->cd", pair_grad, img_unit, preferred_element_type=jnp.float32
        )
        grad_acc = shifted(grad_acc, "blk", 1)
        text_cur = shifted(text_cur, "blk", 1)
        return (text_cur, teach_cur, grad_acc, img_acc, pair_store)

    start_state = (
        txt_unit,
        t_txt_unit,
        jnp.zeros((own_rows, embed_width), jnp.float32),
        jnp.zeros((block_rows, embed_width), jnp.float32),
        pair_start,
    )
    final_state = lax.fori_loop(0, block_count, advance, start_state)
    grad_acc = final_state[2]
    img_acc = final_state[3]
    pair_store = final_state[4]
    img_grad_unit = lax.psum_scatter(
        logit_scale * img_acc, "narrow", scatter_dimension=0, tiled=True
    )
    own_float = lax.dynamic_slice_in_dim(img_float, group_index * own_rows, own_rows, 0)
    own_radius = lax.dynamic_slice_in_dim(img_radius, group_index * own_rows, own_rows, 0)
    image_grad = unit_back(img_grad_unit, own_float, own_radius)
    txt_grad_unit = logit_scale * grad_acc
    text_grad = unit_back(txt_grad_unit, txt_float, txt_radius)
    return (image_grad, text_grad)


def solution(mesh):
    in_specs = (
        P(("blk", "narrow"), None),
        P(("blk", "narrow"), None),
        P(("blk", "narrow"), None),
        P(("blk", "narrow"), None),
    )
    out_specs = (P(("blk", "narrow"), None), P(("blk", "narrow"), None))
    return jax.shard_map(body, mesh=mesh, in_specs=in_specs, out_specs=out_specs, check_vma=False)
```

profile of v0, /device:TPU:1, one launch (start us, length us, event | category | flops | bytes accessed | tf_op | source)
XLA Modules:
  0.0 579.0 jit_solution(6494705080978374956)
XLA Ops:
  14.8 34.3 %all-gather.4.cloned.1.call-done = bf16[1024,1152]{1,0:T(8,128)(2,1)} async-done(((bf16[128,1152]{1,0:T(8,128)(2,1)}), bf16[1024,1152]{1,0:T(8,128)(2,1)}) %all-gather.4.cloned.1.call-update) | async-done | bytes 2359312 | tf_op jit(solution)/shard_map/all_gather | solution.py:34
  55.8 41.1 %all-gather.6.cloned.1.call-done = bf16[1024,1536]{1,0:T(8,128)(2,1)} async-done(((bf16[128,1536]{1,0:T(8,128)(2,1)}), bf16[1024,1536]{1,0:T(8,128)(2,1)}) %all-gather.6.cloned.1.call-update) | async-done | bytes 3145744 | tf_op jit(solution)/shard_map/all_gather | solution.py:35
  99.5 66.9 %all-gather.8.cloned.1.call-done = bf16[2048,1536]{1,0:T(8,128)(2,1)} async-done(((bf16[128,1536]{1,0:T(8,128)(2,1)}), bf16[2048,1536]{1,0:T(8,128)(2,1)}) %all-gather.8.cloned.1.call-update) | async-done | bytes 6291472 | tf_op jit(solution)/shard_map/all_gather | solution.py:49
  166.3 11.8 %multiply_add_fusion = f32[1024,2048]{1,0:T(8,128)} fusion(bf16[2048,1536]{1,0:T(8,128)(2,1)} %all-gather.8.cloned.1.call-done, bf16[1024,1536]{1,0:T(8,128)(2,1)} %all-gather.6.cloned.1.call-done, f32[1024]{0:T(1024)S(1)} %add_sqrt_fusion), kind=kOutput, calls=%fused_computation.15 | convolution fusion | flops 6451363840 | bytes 17829888 | tf_op jit(solution)/shard_map/rd,cd->rc/dot_general | solution.py:46
  178.1 318.0 %while.20 = (s32[]{:T(128)}, bf16[128,1152]{1,0:T(8,128)(2,1)}, f32[128,1152]{1,0:T(8,128)S(1)}, f32[1024,1152]{1,0:T(8,128)}, bf16[1024,1152]{1,0:T(8,128)(2,1)...) while((s32[]{:T(128)}, bf16[128,1152]{1,0:T(8,128)(2,1)}, ...), condition=%wide.region_5.6_spmd.clone, body=%wide.region_4.5_spmd.clone.sunk | while | flops 910442496 | bytes 21365652 | solution.py:87
  186.1 7.0 %collective-permute-done = bf16[128,1152]{1,0:T(8,128)(2,1)} collective-permute-done((bf16[128,1152]{1,0:T(8,128)(2,1)S(1)}, bf16[128,1152]{1,0:T(8,128)(2,1)}, u32[]{:S(2)}, u32[]{:S(2)}) %collective-permute-start) | collective-permute-done | bytes 294944 | tf_op jit(solution)/shard_map/while/body/eval_jaxpr/ppermute | solution.py:13
  201.6 5.3 convolution_add_fusion.5
  258.7 5.3 convolution_add_fusion.5
  297.7 5.3 convolution_add_fusion.5
  303.0 6.5 %collective-permute-done = bf16[128,1152]{1,0:T(8,128)(2,1)} collective-permute-done((bf16[128,1152]{1,0:T(8,128)(2,1)S(1)}, bf16[128,1152]{1,0:T(8,128)(2,1)}, u32[]{:S(2)}, u32[]{:S(2)}) %collective-permute-start) | collective-permute-done | bytes 294944 | tf_op jit(solution)/shard_map/while/body/eval_jaxpr/ppermute | solution.py:13
  322.6 7.7 %collective-permute-done = bf16[128,1152]{1,0:T(8,128)(2,1)} collective-permute-done((bf16[128,1152]{1,0:T(8,128)(2,1)S(1)}, bf16[128,1152]{1,0:T(8,128)(2,1)}, u32[]{:S(2)}, u32[]{:S(2)}) %collective-permute-start) | collective-permute-done | bytes 294944 | tf_op jit(solution)/shard_map/while/body/eval_jaxpr/ppermute | solution.py:13
  336.8 5.3 convolution_add_fusion.5
  342.1 8.9 %collective-permute-done = bf16[128,1152]{1,0:T(8,128)(2,1)} collective-permute-done((bf16[128,1152]{1,0:T(8,128)(2,1)S(1)}, bf16[128,1152]{1,0:T(8,128)(2,1)}, u32[]{:S(2)}, u32[]{:S(2)}) %collective-permute-start) | collective-permute-done | bytes 294944 | tf_op jit(solution)/shard_map/while/body/eval_jaxpr/ppermute | solution.py:13
  361.6 10.1 %collective-permute-done = bf16[128,1152]{1,0:T(8,128)(2,1)} collective-permute-done((bf16[128,1152]{1,0:T(8,128)(2,1)S(1)}, bf16[128,1152]{1,0:T(8,128)(2,1)}, u32[]{:S(2)}, u32[]{:S(2)}) %collective-permute-start) | collective-permute-done | bytes 294944 | tf_op jit(solution)/shard_map/while/body/eval_jaxpr/ppermute | solution.py:13
  376.0 5.3 convolution_add_fusion.5
  381.3 11.1 %collective-permute-done = bf16[128,1152]{1,0:T(8,128)(2,1)} collective-permute-done((bf16[128,1152]{1,0:T(8,128)(2,1)S(1)}, bf16[128,1152]{1,0:T(8,128)(2,1)}, u32[]{:S(2)}, u32[]{:S(2)}) %collective-permute-start) | collective-permute-done | bytes 294944 | tf_op jit(solution)/shard_map/while/body/eval_jaxpr/ppermute | solution.py:13
  396.8 5.3 convolution_add_fusion.5
  402.1 11.1 %collective-permute-done = bf16[128,1152]{1,0:T(8,128)(2,1)} collective-permute-done((bf16[128,1152]{1,0:T(8,128)(2,1)S(1)}, bf16[128,1152]{1,0:T(8,128)(2,1)}, u32[]{:S(2)}, u32[]{:S(2)}) %collective-permute-start) | collective-permute-done | bytes 294944 | tf_op jit(solution)/shard_map/while/body/eval_jaxpr/ppermute | solution.py:13
  422.8 11.1 %collective-permute-done = bf16[128,1152]{1,0:T(8,128)(2,1)} collective-permute-done((bf16[128,1152]{1,0:T(8,128)(2,1)S(1)}, bf16[128,1152]{1,0:T(8,128)(2,1)}, u32[]{:S(2)}, u32[]{:S(2)}) %collective-permute-start) | collective-permute-done | bytes 294944 | tf_op jit(solution)/shard_map/while/body/eval_jaxpr/ppermute | solution.py:13
  438.3 5.3 convolution_add_fusion.5
  443.5 11.1 %collective-permute-done = bf16[128,1152]{1,0:T(8,128)(2,1)} collective-permute-done((bf16[128,1152]{1,0:T(8,128)(2,1)S(1)}, bf16[128,1152]{1,0:T(8,128)(2,1)}, u32[]{:S(2)}, u32[]{:S(2)}) %collective-permute-start) | collective-permute-done | bytes 294944 | tf_op jit(solution)/shard_map/while/body/eval_jaxpr/ppermute | solution.py:13
  464.3 11.1 %collective-permute-done = bf16[128,1152]{1,0:T(8,128)(2,1)} collective-permute-done((bf16[128,1152]{1,0:T(8,128)(2,1)S(1)}, bf16[128,1152]{1,0:T(8,128)(2,1)}, u32[]{:S(2)}, u32[]{:S(2)}) %collective-permute-start) | collective-permute-done | bytes 294944 | tf_op jit(solution)/shard_map/while/body/eval_jaxpr/ppermute | solution.py:13
  485.0 11.1 %collective-permute-done = bf16[128,1152]{1,0:T(8,128)(2,1)} collective-permute-done((bf16[128,1152]{1,0:T(8,128)(2,1)S(1)}, bf16[128,1152]{1,0:T(8,128)(2,1)}, u32[]{:S(2)}, u32[]{:S(2)}) %collective-permute-start) | collective-permute-done | bytes 294944 | tf_op jit(solution)/shard_map/while/body/eval_jaxpr/ppermute | solution.py:13
  503.1 65.7 %reduce-scatter.2.cloned.1.call-done = f32[128,1152]{1,0:T(8,128)} async-done(((f32[1024,1152]{1,0:T(8,128)}), f32[128,1152]{1,0:T(8,128)}) %reduce-scatter.2.cloned.1.call-update) | async-done | bytes 589840 | tf_op jit(solution)/shard_map/reduce_scatter | solution.py:91
  (140 shorter events, 201.5 us)
Async XLA Ops:
  7.2 41.9 %all-gather.4.cloned.1.call-start = ((), (), s32[]{:S(2)}) async-start(), calls=%async_computation.1 | async-start | bytes 2654208 | tf_op jit(solution)/shard_map/all_gather | solution.py:34
  7.9 89.0 %all-gather.6.cloned.1.call-start = ((), (), s32[]{:S(2)}) async-start(), calls=%async_computation.2 | async-start | bytes 3538944 | tf_op jit(solution)/shard_map/all_gather | solution.py:35
  8.6 157.7 %all-gather.8.cloned.1.call-start = ((), (), s32[]{:S(2)}) async-start(), calls=%async_computation.3 | async-start | bytes 6684672 | tf_op jit(solution)/shard_map/all_gather | solution.py:49
  11.8 557.1 %reduce-scatter.2.cloned.1.call-start = ((), (), s32[]{:S(2)}) async-start(), calls=%async_computation.4 | async-start | bytes 5308416 | tf_op jit(solution)/shard_map/reduce_scatter | solution.py:91
  272.3 16.4 %collective-permute-start.1 = (f32[128,1152]{1,0:T(8,128)}, f32[128,1152]{1,0:T(8,128)S(1)}, u32[]{:S(2)}, u32[]{:S(2)}) collective-permute-start(f32[128,1152]{1,0:T(8,128)} %convolution_add_fusion.4), channel_id=1, source_target_pairs={{0,8},{8,16},{16,24},{24,32},{32,40},{40,48},{48,56},{56,64},{64,7... | collective-permute-start | bytes 1769480 | tf_op jit(solution)/shard_map/while/body/eval_jaxpr/ppermute | solution.py:13
  293.1 16.4 %collective-permute-start.1 = (f32[128,1152]{1,0:T(8,128)}, f32[128,1152]{1,0:T(8,128)S(1)}, u32[]{:S(2)}, u32[]{:S(2)}) collective-permute-start(f32[128,1152]{1,0:T(8,128)} %convolution_add_fusion.4), channel_id=1, source_target_pairs={{0,8},{8,16},{16,24},{24,32},{32,40},{40,48},{48,56},{56,64},{64,7... | collective-permute-start | bytes 1769480 | tf_op jit(solution)/shard_map/while/body/eval_jaxpr/ppermute | solution.py:13
  313.8 16.4 %collective-permute-start.1 = (f32[128,1152]{1,0:T(8,128)}, f32[128,1152]{1,0:T(8,128)S(1)}, u32[]{:S(2)}, u32[]{:S(2)}) collective-permute-start(f32[128,1152]{1,0:T(8,128)} %convolution_add_fusion.4), channel_id=1, source_target_pairs={{0,8},{8,16},{16,24},{24,32},{32,40},{40,48},{48,56},{56,64},{64,7... | collective-permute-start | bytes 1769480 | tf_op jit(solution)/shard_map/while/body/eval_jaxpr/ppermute | solution.py:13
  313.8 16.4 %collective-permute-start = (bf16[128,1152]{1,0:T(8,128)(2,1)S(1)}, bf16[128,1152]{1,0:T(8,128)(2,1)}, u32[]{:S(2)}, u32[]{:S(2)}) collective-permute-start(bf16[128,1152]{1,0:T(8,128)(2,1)S(1)} %copy.11), channel_id=1, source_target_pairs={{0,8},{8,16},{16,24},{24,32},{32,40},{40,48},{48,56},{56,64},{64,7... | collective-permute-start | bytes 884744 | tf_op jit(solution)/shard_map/while/body/eval_jaxpr/ppermute | solution.py:13
  334.6 16.4 %collective-permute-start.1 = (f32[128,1152]{1,0:T(8,128)}, f32[128,1152]{1,0:T(8,128)S(1)}, u32[]{:S(2)}, u32[]{:S(2)}) collective-permute-start(f32[128,1152]{1,0:T(8,128)} %convolution_add_fusion.4), channel_id=1, source_target_pairs={{0,8},{8,16},{16,24},{24,32},{32,40},{40,48},{48,56},{56,64},{64,7... | collective-permute-start | bytes 1769480 | tf_op jit(solution)/shard_map/while/body/eval_jaxpr/ppermute | solution.py:13
  334.6 16.4 %collective-permute-start = (bf16[128,1152]{1,0:T(8,128)(2,1)S(1)}, bf16[128,1152]{1,0:T(8,128)(2,1)}, u32[]{:S(2)}, u32[]{:S(2)}) collective-permute-start(bf16[128,1152]{1,0:T(8,128)(2,1)S(1)} %copy.11), channel_id=1, source_target_pairs={{0,8},{8,16},{16,24},{24,32},{32,40},{40,48},{48,56},{56,64},{64,7... | collective-permute-start | bytes 884744 | tf_op jit(solution)/shard_map/while/body/eval_jaxpr/ppermute | solution.py:13
  355.3 16.4 %collective-permute-start.1 = (f32[128,1152]{1,0:T(8,128)}, f32[128,1152]{1,0:T(8,128)S(1)}, u32[]{:S(2)}, u32[]{:S(2)}) collective-permute-start(f32[128,1152]{1,0:T(8,128)} %convolution_add_fusion.4), channel_id=1, source_target_pairs={{0,8},{8,16},{16,24},{24,32},{32,40},{40,48},{48,56},{56,64},{64,7... | collective-permute-start | bytes 1769480 | tf_op jit(solution)/shard_map/while/body/eval_jaxpr/ppermute | solution.py:13
  355.3 16.4 %collective-permute-start = (bf16[128,1152]{1,0:T(8,128)(2,1)S(1)}, bf16[128,1152]{1,0:T(8,128)(2,1)}, u32[]{:S(2)}, u32[]{:S(2)}) collective-permute-start(bf16[128,1152]{1,0:T(8,128)(2,1)S(1)} %copy.11), channel_id=1, source_target_pairs={{0,8},{8,16},{16,24},{24,32},{32,40},{40,48},{48,56},{56,64},{64,7... | collective-permute-start | bytes 884744 | tf_op jit(solution)/shard_map/while/body/eval_jaxpr/ppermute | solution.py:13
  376.0 16.4 %collective-permute-start.1 = (f32[128,1152]{1,0:T(8,128)}, f32[128,1152]{1,0:T(8,128)S(1)}, u32[]{:S(2)}, u32[]{:S(2)}) collective-permute-start(f32[128,1152]{1,0:T(8,128)} %convolution_add_fusion.4), channel_id=1, source_target_pairs={{0,8},{8,16},{16,24},{24,32},{32,40},{40,48},{48,56},{56,64},{64,7... | collective-permute-start | bytes 1769480 | tf_op jit(solution)/shard_map/while/body/eval_jaxpr/ppermute | solution.py:13
  376.0 16.4 %collective-permute-start = (bf16[128,1152]{1,0:T(8,128)(2,1)S(1)}, bf16[128,1152]{1,0:T(8,128)(2,1)}, u32[]{:S(2)}, u32[]{:S(2)}) collective-permute-start(bf16[128,1152]{1,0:T(8,128)(2,1)S(1)} %copy.11), channel_id=1, source_target_pairs={{0,8},{8,16},{16,24},{24,32},{32,40},{40,48},{48,56},{56,64},{64,7... | collective-permute-start | bytes 884744 | tf_op jit(solution)/shard_map/while/body/eval_jaxpr/ppermute | solution.py:13
  396.8 16.4 %collective-permute-start.1 = (f32[128,1152]{1,0:T(8,128)}, f32[128,1152]{1,0:T(8,128)S(1)}, u32[]{:S(2)}, u32[]{:S(2)}) collective-permute-start(f32[128,1152]{1,0:T(8,128)} %convolution_add_fusion.4), channel_id=1, source_target_pairs={{0,8},{8,16},{16,24},{24,32},{32,40},{40,48},{48,56},{56,64},{64,7... | collective-permute-start | bytes 1769480 | tf_op jit(solution)/shard_map/while/body/eval_jaxpr/ppermute | solution.py:13
  396.8 16.4 %collective-permute-start = (bf16[128,1152]{1,0:T(8,128)(2,1)S(1)}, bf16[128,1152]{1,0:T(8,128)(2,1)}, u32[]{:S(2)}, u32[]{:S(2)}) collective-permute-start(bf16[128,1152]{1,0:T(8,128)(2,1)S(1)} %copy.11), channel_id=1, source_target_pairs={{0,8},{8,16},{16,24},{24,32},{32,40},{40,48},{48,56},{56,64},{64,7... | collective-permute-start | bytes 884744 | tf_op jit(solution)/shard_map/while/body/eval_jaxpr/ppermute | solution.py:13
  417.5 16.4 %collective-permute-start.1 = (f32[128,1152]{1,0:T(8,128)}, f32[128,1152]{1,0:T(8,128)S(1)}, u32[]{:S(2)}, u32[]{:S(2)}) collective-permute-start(f32[128,1152]{1,0:T(8,128)} %convolution_add_fusion.4), channel_id=1, source_target_pairs={{0,8},{8,16},{16,24},{24,32},{32,40},{40,48},{48,56},{56,64},{64,7... | collective-permute-start | bytes 1769480 | tf_op jit(solution)/shard_map/while/body/eval_jaxpr/ppermute | solution.py:13
  417.5 16.4 %collective-permute-start = (bf16[128,1152]{1,0:T(8,128)(2,1)S(1)}, bf16[128,1152]{1,0:T(8,128)(2,1)}, u32[]{:S(2)}, u32[]{:S(2)}) collective-permute-start(bf16[128,1152]{1,0:T(8,128)(2,1)S(1)} %copy.11), channel_id=1, source_target_pairs={{0,8},{8,16},{16,24},{24,32},{32,40},{40,48},{48,56},{56,64},{64,7... | collective-permute-start | bytes 884744 | tf_op jit(solution)/shard_map/while/body/eval_jaxpr/ppermute | solution.py:13
  438.3 16.4 %collective-permute-start.1 = (f32[128,1152]{1,0:T(8,128)}, f32[128,1152]{1,0:T(8,128)S(1)}, u32[]{:S(2)}, u32[]{:S(2)}) collective-permute-start(f32[128,1152]{1,0:T(8,128)} %convolution_add_fusion.4), channel_id=1, source_target_pairs={{0,8},{8,16},{16,24},{24,32},{32,40},{40,48},{48,56},{56,64},{64,7... | collective-permute-start | bytes 1769480 | tf_op jit(solution)/shard_map/while/body/eval_jaxpr/ppermute | solution.py:13
  438.3 16.4 %collective-permute-start = (bf16[128,1152]{1,0:T(8,128)(2,1)S(1)}, bf16[128,1152]{1,0:T(8,128)(2,1)}, u32[]{:S(2)}, u32[]{:S(2)}) collective-permute-start(bf16[128,1152]{1,0:T(8,128)(2,1)S(1)} %copy.11), channel_id=1, source_target_pairs={{0,8},{8,16},{16,24},{24,32},{32,40},{40,48},{48,56},{56,64},{64,7... | collective-permute-start | bytes 884744 | tf_op jit(solution)/shard_map/while/body/eval_jaxpr/ppermute | solution.py:13
  459.0 16.4 %collective-permute-start.1 = (f32[128,1152]{1,0:T(8,128)}, f32[128,1152]{1,0:T(8,128)S(1)}, u32[]{:S(2)}, u32[]{:S(2)}) collective-permute-start(f32[128,1152]{1,0:T(8,128)} %convolution_add_fusion.4), channel_id=1, source_target_pairs={{0,8},{8,16},{16,24},{24,32},{32,40},{40,48},{48,56},{56,64},{64,7... | collective-permute-start | bytes 1769480 | tf_op jit(solution)/shard_map/while/body/eval_jaxpr/ppermute | solution.py:13
  459.0 16.4 %collective-permute-start = (bf16[128,1152]{1,0:T(8,128)(2,1)S(1)}, bf16[128,1152]{1,0:T(8,128)(2,1)}, u32[]{:S(2)}, u32[]{:S(2)}) collective-permute-start(bf16[128,1152]{1,0:T(8,128)(2,1)S(1)} %copy.11), channel_id=1, source_target_pairs={{0,8},{8,16},{16,24},{24,32},{32,40},{40,48},{48,56},{56,64},{64,7... | collective-permute-start | bytes 884744 | tf_op jit(solution)/shard_map/while/body/eval_jaxpr/ppermute | solution.py:13
  479.7 16.4 %collective-permute-start.1 = (f32[128,1152]{1,0:T(8,128)}, f32[128,1152]{1,0:T(8,128)S(1)}, u32[]{:S(2)}, u32[]{:S(2)}) collective-permute-start(f32[128,1152]{1,0:T(8,128)} %convolution_add_fusion.4), channel_id=1, source_target_pairs={{0,8},{8,16},{16,24},{24,32},{32,40},{40,48},{48,56},{56,64},{64,7... | collective-permute-start | bytes 1769480 | tf_op jit(solution)/shard_map/while/body/eval_jaxpr/ppermute | solution.py:13
  479.7 16.4 %collective-permute-start = (bf16[128,1152]{1,0:T(8,128)(2,1)S(1)}, bf16[128,1152]{1,0:T(8,128)(2,1)}, u32[]{:S(2)}, u32[]{:S(2)}) collective-permute-start(bf16[128,1152]{1,0:T(8,128)(2,1)S(1)} %copy.11), channel_id=1, source_target_pairs={{0,8},{8,16},{16,24},{24,32},{32,40},{40,48},{48,56},{56,64},{64,7... | collective-permute-start | bytes 884744 | tf_op jit(solution)/shard_map/while/body/eval_jaxpr/ppermute | solution.py:13
  (13 other events, 147.9 us)
Sparse Core Ops, SparseCore 0:
  9.6 39.4 all-gather.3
  50.7 46.1 all-gather.5
  99.9 66.3 all-gather.7
  501.1 67.7 reduce-scatter.1
where the time goes:
time: 581 us; the launch traced here: 579 us
  waiting for transfers between devices  340 us (59%)
  matrix products  148 us (25%)
  starting transfers between devices  36.1 us (6%)
  other arithmetic  24.9 us (4%)
  local copies, waits for them, and re-layouts  16.4 us (3%)
  between operations  13.8 us (2%)
    ppermute x32, waiting for transfers between devices, shifted(): return lax.ppermute(x, axis, [(i, (i + by) % count) for i in range(count)])  130 us
    dot_general x16, matrix products, advance(): jnp.dot(pair_grad, text_cur, preferred_element_type=jnp.float32)  82.2 us
    all_gather x1, waiting for transfers between devices, body(): lax.all_gather(t_txt_unit, 'blk', axis=0, tiled=True)  66.9 us
    reduce_scatter x1, waiting for transfers between devices, body(): lax.psum_scatter(logit_scale * img_acc, 'narrow', scatter_dimension=0, ti...  65.7 us
    all_gather x1, waiting for transfers between devices, body(): lax.all_gather(teacher_img, 'narrow', axis=0, tiled=True)  41.1 us
    ppermute x32, starting transfers between devices, shifted(): return lax.ppermute(x, axis, [(i, (i + by) % count) for i in range(count)])  36 us
    all_gather x1, waiting for transfers between devices, body(): lax.all_gather(student_img, 'narrow', axis=0, tiled=True)  34.3 us
    dot_general x16, matrix products, advance(): jnp.einsum('rd,cd->rc', img_unit, text_cur, preferred_element_type=jnp.fl...  32.1 us
  transfers between devices with their start and end apart: 36, of which 20 were waited for; matrix products, arithmetic and copies ran while one was open for 17% of the time, Pallas kernels for 0%

commit v1 on v0

--- a/solution.py
+++ b/solution.py
@@ -46,7 +46,9 @@
         * jnp.einsum(
             "rd,cd->rc",
             t_img_unit,
-            lax.all_gather(t_txt_unit, "blk", axis=0, tiled=True),
+            jnp.concatenate(
+                lax.all_to_all(jnp.stack([t_txt_unit] * lax.axis_size("blk")), "blk", 0, 0), axis=0
+            ),
             preferred_element_type=jnp.float32,
         )
         + logit_bias

time: 581 us -> 561 us (0.966)
  waiting for transfers between devices: 340 us -> 313 us
  starting transfers between devices: 36.1 us -> 42.6 us
    all_gather x1 -> x0, waiting for transfers between devices: 66.9 us -> none  [body(): lax.all_gather(t_txt_unit, 'blk', axis=0, tiled=True)]
    all_gather x1, waiting for transfers between devices: 41.1 us -> 67.6 us  [body(): lax.all_gather(teacher_img, 'narrow', axis=0, tiled=True)]
    all_to_all x0 -> x1, starting transfers between devices: none -> 9.41 us  [body(): lax.all_to_all(jnp.stack([t_txt_unit] * lax.axis_size('blk')), 'blk', 0, 0)]
    all_gather x1, waiting for transfers between devices: 34.3 us -> 42.8 us  [body(): lax.all_gather(student_img, 'narrow', axis=0, tiled=True)]
  transfers between devices with their start and end apart: 36 -> 36, of which waited for: 20 -> 20; matrix products, arithmetic and copies ran while one was open for 17% -> 18% of each run, Pallas kernels for 0% -> 0%
where the time goes in v1:
time: 561 us; the launch traced here: 559 us
  waiting for transfers between devices  313 us (56%)
  matrix products  148 us (26%)
  starting transfers between devices  42.6 us (8%)
  other arithmetic  22.2 us (4%)
  local copies, waits for them, and re-layouts  19.7 us (4%)
  between operations  13.8 us (2%)
    ppermute x32, waiting for transfers between devices, shifted(): return lax.ppermute(x, axis, [(i, (i + by) % count) for i in range(count)])  134 us
    dot_general x16, matrix products, advance(): jnp.dot(pair_grad, text_cur, preferred_element_type=jnp.float32)  82.2 us
    all_gather x1, waiting for transfers between devices, body(): lax.all_gather(teacher_img, 'narrow', axis=0, tiled=True)  67.6 us
    reduce_scatter x1, waiting for transfers between devices, body(): lax.psum_scatter(logit_scale * img_acc, 'narrow', scatter_dimension=0, ti...  65.4 us
    all_gather x1, waiting for transfers between devices, body(): lax.all_gather(student_img, 'narrow', axis=0, tiled=True)  42.8 us
    ppermute x32, starting transfers between devices, shifted(): return lax.ppermute(x, axis, [(i, (i + by) % count) for i in range(count)])  33 us
    dot_general x16, matrix products, advance(): jnp.einsum('rd,cd->rc', img_unit, text_cur, preferred_element_type=jnp.fl...  32.1 us
    dot_general x16, matrix products, advance(): jnp.einsum('rc,rd->cd', pair_grad, img_unit, preferred_element_type=jnp.f...  21.8 us
  transfers between devices with their start and end apart: 36, of which 20 were waited for; matrix products, arithmetic and copies ran while one was open for 18% of the time, Pallas kernels for 0%

profile of v1, /device:TPU:1, one launch (start us, length us, event | category | flops | bytes accessed | tf_op | source)
XLA Modules:
  0.0 559.0 jit_solution(9135489168293927808)
XLA Ops:
  14.2 9.4 %all-to-all-start = ((bf16[16,128,1536]{2,1,0:T(8,128)(2,1)}), bf16[16,128,1536]{2,1,0:T(8,128)(2,1)}, u32[]{:S(2)}, u32[]{:S(2)}) async-start(bf16[16,128,1536]{2,1,0:T(8,128)(2,1)} %stack.2), calls=%async_computation | async-start | bytes 12582912 | tf_op jit(solution)/shard_map/all_to_all | solution.py:50
  24.7 42.8 %all-gather.3.cloned.1.call-done = bf16[1024,1152]{1,0:T(8,128)(2,1)} async-done(((bf16[128,1152]{1,0:T(8,128)(2,1)}), bf16[1024,1152]{1,0:T(8,128)(2,1)}) %all-gather.3.cloned.1.call-update) | async-done | bytes 2359312 | tf_op jit(solution)/shard_map/all_gather | solution.py:34
  74.2 67.6 %all-gather.5.cloned.1.call-done = bf16[1024,1536]{1,0:T(8,128)(2,1)} async-done(((bf16[128,1536]{1,0:T(8,128)(2,1)}), bf16[1024,1536]{1,0:T(8,128)(2,1)}) %all-gather.5.cloned.1.call-update) | async-done | bytes 3145744 | tf_op jit(solution)/shard_map/all_gather | solution.py:35
  146.4 11.8 %multiply_add_fusion = f32[1024,2048]{1,0:T(8,128)} fusion(bf16[2048,1536]{1,0:T(8,128)(2,1)} %bitcast, bf16[1024,1536]{1,0:T(8,128)(2,1)} %all-gather.5.cloned.1.call-done, f32[1024]{0:T(1024)S(1)} %add_sqrt_fusion), kind=kOutput, calls=%fused_computation.15 | convolution fusion | flops 6451363840 | bytes 17829888 | tf_op jit(solution)/shard_map/rd,cd->rc/dot_general | solution.py:46
  158.2 318.4 %while.20 = (s32[]{:T(128)}, bf16[128,1152]{1,0:T(8,128)(2,1)}, f32[128,1152]{1,0:T(8,128)S(1)}, f32[1024,1152]{1,0:T(8,128)}, bf16[1024,1152]{1,0:T(8,128)(2,1)...) while((s32[]{:T(128)}, bf16[128,1152]{1,0:T(8,128)(2,1)}, ...), condition=%wide.region_5.6_spmd.clone, body=%wide.region_4.5_spmd.clone.sunk | while | flops 910442496 | bytes 21365652 | solution.py:89
  166.5 7.2 %collective-permute-done = bf16[128,1152]{1,0:T(8,128)(2,1)} collective-permute-done((bf16[128,1152]{1,0:T(8,128)(2,1)S(1)}, bf16[128,1152]{1,0:T(8,128)(2,1)}, u32[]{:S(2)}, u32[]{:S(2)}) %collective-permute-start) | collective-permute-done | bytes 294944 | tf_op jit(solution)/shard_map/while/body/eval_jaxpr/ppermute | solution.py:13
  238.6 5.3 convolution_add_fusion.5
  263.4 5.7 %collective-permute-done = bf16[128,1152]{1,0:T(8,128)(2,1)} collective-permute-done((bf16[128,1152]{1,0:T(8,128)(2,1)S(1)}, bf16[128,1152]{1,0:T(8,128)(2,1)}, u32[]{:S(2)}, u32[]{:S(2)}) %collective-permute-start) | collective-permute-done | bytes 294944 | tf_op jit(solution)/shard_map/while/body/eval_jaxpr/ppermute | solution.py:13
  277.7 5.3 convolution_add_fusion.5
  283.0 6.9 %collective-permute-done = bf16[128,1152]{1,0:T(8,128)(2,1)} collective-permute-done((bf16[128,1152]{1,0:T(8,128)(2,1)S(1)}, bf16[128,1152]{1,0:T(8,128)(2,1)}, u32[]{:S(2)}, u32[]{:S(2)}) %collective-permute-start) | collective-permute-done | bytes 294944 | tf_op jit(solution)/shard_map/while/body/eval_jaxpr/ppermute | solution.py:13
  302.5 8.1 %collective-permute-done = bf16[128,1152]{1,0:T(8,128)(2,1)} collective-permute-done((bf16[128,1152]{1,0:T(8,128)(2,1)S(1)}, bf16[128,1152]{1,0:T(8,128)(2,1)}, u32[]{:S(2)}, u32[]{:S(2)}) %collective-permute-start) | collective-permute-done | bytes 294944 | tf_op jit(solution)/shard_map/while/body/eval_jaxpr/ppermute | solution.py:13
  316.7 5.3 convolution_add_fusion.5
  322.0 9.3 %collective-permute-done = bf16[128,1152]{1,0:T(8,128)(2,1)} collective-permute-done((bf16[128,1152]{1,0:T(8,128)(2,1)S(1)}, bf16[128,1152]{1,0:T(8,128)(2,1)}, u32[]{:S(2)}, u32[]{:S(2)}) %collective-permute-start) | collective-permute-done | bytes 294944 | tf_op jit(solution)/shard_map/while/body/eval_jaxpr/ppermute | solution.py:13
  341.5 10.6 %collective-permute-done = bf16[128,1152]{1,0:T(8,128)(2,1)} collective-permute-done((bf16[128,1152]{1,0:T(8,128)(2,1)S(1)}, bf16[128,1152]{1,0:T(8,128)(2,1)}, u32[]{:S(2)}, u32[]{:S(2)}) %collective-permute-start) | collective-permute-done | bytes 294944 | tf_op jit(solution)/shard_map/while/body/eval_jaxpr/ppermute | solution.py:13
  356.4 5.3 convolution_add_fusion.5
  361.7 11.1 %collective-permute-done = bf16[128,1152]{1,0:T(8,128)(2,1)} collective-permute-done((bf16[128,1152]{1,0:T(8,128)(2,1)S(1)}, bf16[128,1152]{1,0:T(8,128)(2,1)}, u32[]{:S(2)}, u32[]{:S(2)}) %collective-permute-start) | collective-permute-done | bytes 294944 | tf_op jit(solution)/shard_map/while/body/eval_jaxpr/ppermute | solution.py:13
  377.2 5.3 convolution_add_fusion.5
  382.4 11.1 %collective-permute-done = bf16[128,1152]{1,0:T(8,128)(2,1)} collective-permute-done((bf16[128,1152]{1,0:T(8,128)(2,1)S(1)}, bf16[128,1152]{1,0:T(8,128)(2,1)}, u32[]{:S(2)}, u32[]{:S(2)}) %collective-permute-start) | collective-permute-done | bytes 294944 | tf_op jit(solution)/shard_map/while/body/eval_jaxpr/ppermute | solution.py:13
  403.2 11.1 %collective-permute-done = bf16[128,1152]{1,0:T(8,128)(2,1)} collective-permute-done((bf16[128,1152]{1,0:T(8,128)(2,1)S(1)}, bf16[128,1152]{1,0:T(8,128)(2,1)}, u32[]{:S(2)}, u32[]{:S(2)}) %collective-permute-start) | collective-permute-done | bytes 294944 | tf_op jit(solution)/shard_map/while/body/eval_jaxpr/ppermute | solution.py:13
  423.9 11.1 %collective-permute-done = bf16[128,1152]{1,0:T(8,128)(2,1)} collective-permute-done((bf16[128,1152]{1,0:T(8,128)(2,1)S(1)}, bf16[128,1152]{1,0:T(8,128)(2,1)}, u32[]{:S(2)}, u32[]{:S(2)}) %collective-permute-start) | collective-permute-done | bytes 294944 | tf_op jit(solution)/shard_map/while/body/eval_jaxpr/ppermute | solution.py:13
  439.4 5.3 convolution_add_fusion.5
  444.7 11.1 %collective-permute-done = bf16[128,1152]{1,0:T(8,128)(2,1)} collective-permute-done((bf16[128,1152]{1,0:T(8,128)(2,1)S(1)}, bf16[128,1152]{1,0:T(8,128)(2,1)}, u32[]{:S(2)}, u32[]{:S(2)}) %collective-permute-start) | collective-permute-done | bytes 294944 | tf_op jit(solution)/shard_map/while/body/eval_jaxpr/ppermute | solution.py:13
  465.4 11.1 %collective-permute-done = bf16[128,1152]{1,0:T(8,128)(2,1)} collective-permute-done((bf16[128,1152]{1,0:T(8,128)(2,1)S(1)}, bf16[128,1152]{1,0:T(8,128)(2,1)}, u32[]{:S(2)}, u32[]{:S(2)}) %collective-permute-start) | collective-permute-done | bytes 294944 | tf_op jit(solution)/shard_map/while/body/eval_jaxpr/ppermute | solution.py:13
  483.5 65.4 %reduce-scatter.2.cloned.1.call-done = f32[128,1152]{1,0:T(8,128)} async-done(((f32[1024,1152]{1,0:T(8,128)}), f32[128,1152]{1,0:T(8,128)}) %reduce-scatter.2.cloned.1.call-update) | async-done | bytes 589840 | tf_op jit(solution)/shard_map/reduce_scatter | solution.py:93
  (142 shorter events, 201.9 us)
Async XLA Ops:
  7.2 60.3 %all-gather.3.cloned.1.call-start = ((), (), s32[]{:S(2)}) async-start(), calls=%async_computation.2 | async-start | bytes 2654208 | tf_op jit(solution)/shard_map/all_gather | solution.py:34
  7.9 133.9 %all-gather.5.cloned.1.call-start = ((), (), s32[]{:S(2)}) async-start(), calls=%async_computation.3 | async-start | bytes 3538944 | tf_op jit(solution)/shard_map/all_gather | solution.py:35
  14.2 132.2 %all-to-all-start = ((bf16[16,128,1536]{2,1,0:T(8,128)(2,1)}), bf16[16,128,1536]{2,1,0:T(8,128)(2,1)}, u32[]{:S(2)}, u32[]{:S(2)}) async-start(bf16[16,128,1536]{2,1,0:T(8,128)(2,1)} %stack.2), calls=%async_computation | async-start | bytes 12582912 | tf_op jit(solution)/shard_map/all_to_all | solution.py:50
  23.6 525.3 %reduce-scatter.2.cloned.1.call-start = ((), (), s32[]{:S(2)}) async-start(), calls=%async_computation.4 | async-start | bytes 5308416 | tf_op jit(solution)/shard_map/reduce_scatter | solution.py:93
  252.7 16.4 %collective-permute-start.1 = (f32[128,1152]{1,0:T(8,128)}, f32[128,1152]{1,0:T(8,128)S(1)}, u32[]{:S(2)}, u32[]{:S(2)}) collective-permute-start(f32[128,1152]{1,0:T(8,128)} %convolution_add_fusion.4), channel_id=1, source_target_pairs={{0,8},{8,16},{16,24},{24,32},{32,40},{40,48},{48,56},{56,64},{64,7... | collective-permute-start | bytes 1769480 | tf_op jit(solution)/shard_map/while/body/eval_jaxpr/ppermute | solution.py:13
  273.5 16.4 %collective-permute-start.1 = (f32[128,1152]{1,0:T(8,128)}, f32[128,1152]{1,0:T(8,128)S(1)}, u32[]{:S(2)}, u32[]{:S(2)}) collective-permute-start(f32[128,1152]{1,0:T(8,128)} %convolution_add_fusion.4), channel_id=1, source_target_pairs={{0,8},{8,16},{16,24},{24,32},{32,40},{40,48},{48,56},{56,64},{64,7... | collective-permute-start | bytes 1769480 | tf_op jit(solution)/shard_map/while/body/eval_jaxpr/ppermute | solution.py:13
  294.2 16.4 %collective-permute-start.1 = (f32[128,1152]{1,0:T(8,128)}, f32[128,1152]{1,0:T(8,128)S(1)}, u32[]{:S(2)}, u32[]{:S(2)}) collective-permute-start(f32[128,1152]{1,0:T(8,128)} %convolution_add_fusion.4), channel_id=1, source_target_pairs={{0,8},{8,16},{16,24},{24,32},{32,40},{40,48},{48,56},{56,64},{64,7... | collective-permute-start | bytes 1769480 | tf_op jit(solution)/shard_map/while/body/eval_jaxpr/ppermute | solution.py:13
  294.2 16.4 %collective-permute-start = (bf16[128,1152]{1,0:T(8,128)(2,1)S(1)}, bf16[128,1152]{1,0:T(8,128)(2,1)}, u32[]{:S(2)}, u32[]{:S(2)}) collective-permute-start(bf16[128,1152]{1,0:T(8,128)(2,1)S(1)} %copy.11), channel_id=1, source_target_pairs={{0,8},{8,16},{16,24},{24,32},{32,40},{40,48},{48,56},{56,64},{64,7... | collective-permute-start | bytes 884744 | tf_op jit(solution)/shard_map/while/body/eval_jaxpr/ppermute | solution.py:13
  314.9 16.4 %collective-permute-start.1 = (f32[128,1152]{1,0:T(8,128)}, f32[128,1152]{1,0:T(8,128)S(1)}, u32[]{:S(2)}, u32[]{:S(2)}) collective-permute-start(f32[128,1152]{1,0:T(8,128)} %convolution_add_fusion.4), channel_id=1, source_target_pairs={{0,8},{8,16},{16,24},{24,32},{32,40},{40,48},{48,56},{56,64},{64,7... | collective-permute-start | bytes 1769480 | tf_op jit(solution)/shard_map/while/body/eval_jaxpr/ppermute | solution.py:13
  314.9 16.4 %collective-permute-start = (bf16[128,1152]{1,0:T(8,128)(2,1)S(1)}, bf16[128,1152]{1,0:T(8,128)(2,1)}, u32[]{:S(2)}, u32[]{:S(2)}) collective-permute-start(bf16[128,1152]{1,0:T(8,128)(2,1)S(1)} %copy.11), channel_id=1, source_target_pairs={{0,8},{8,16},{16,24},{24,32},{32,40},{40,48},{48,56},{56,64},{64,7... | collective-permute-start | bytes 884744 | tf_op jit(solution)/shard_map/while/body/eval_jaxpr/ppermute | solution.py:13
  335.7 16.4 %collective-permute-start.1 = (f32[128,1152]{1,0:T(8,128)}, f32[128,1152]{1,0:T(8,128)S(1)}, u32[]{:S(2)}, u32[]{:S(2)}) collective-permute-start(f32[128,1152]{1,0:T(8,128)} %convolution_add_fusion.4), channel_id=1, source_target_pairs={{0,8},{8,16},{16,24},{24,32},{32,40},{40,48},{48,56},{56,64},{64,7... | collective-permute-start | bytes 1769480 | tf_op jit(solution)/shard_map/while/body/eval_jaxpr/ppermute | solution.py:13
  335.7 16.4 %collective-permute-start = (bf16[128,1152]{1,0:T(8,128)(2,1)S(1)}, bf16[128,1152]{1,0:T(8,128)(2,1)}, u32[]{:S(2)}, u32[]{:S(2)}) collective-permute-start(bf16[128,1152]{1,0:T(8,128)(2,1)S(1)} %copy.11), channel_id=1, source_target_pairs={{0,8},{8,16},{16,24},{24,32},{32,40},{40,48},{48,56},{56,64},{64,7... | collective-permute-start | bytes 884744 | tf_op jit(solution)/shard_map/while/body/eval_jaxpr/ppermute | solution.py:13
  356.4 16.4 %collective-permute-start.1 = (f32[128,1152]{1,0:T(8,128)}, f32[128,1152]{1,0:T(8,128)S(1)}, u32[]{:S(2)}, u32[]{:S(2)}) collective-permute-start(f32[128,1152]{1,0:T(8,128)} %convolution_add_fusion.4), channel_id=1, source_target_pairs={{0,8},{8,16},{16,24},{24,32},{32,40},{40,48},{48,56},{56,64},{64,7... | collective-permute-start | bytes 1769480 | tf_op jit(solution)/shard_map/while/body/eval_jaxpr/ppermute | solution.py:13
  356.4 16.4 %collective-permute-start = (bf16[128,1152]{1,0:T(8,128)(2,1)S(1)}, bf16[128,1152]{1,0:T(8,128)(2,1)}, u32[]{:S(2)}, u32[]{:S(2)}) collective-permute-start(bf16[128,1152]{1,0:T(8,128)(2,1)S(1)} %copy.11), channel_id=1, source_target_pairs={{0,8},{8,16},{16,24},{24,32},{32,40},{40,48},{48,56},{56,64},{64,7... | collective-permute-start | bytes 884744 | tf_op jit(solution)/shard_map/while/body/eval_jaxpr/ppermute | solution.py:13
  377.2 16.4 %collective-permute-start.1 = (f32[128,1152]{1,0:T(8,128)}, f32[128,1152]{1,0:T(8,128)S(1)}, u32[]{:S(2)}, u32[]{:S(2)}) collective-permute-start(f32[128,1152]{1,0:T(8,128)} %convolution_add_fusion.4), channel_id=1, source_target_pairs={{0,8},{8,16},{16,24},{24,32},{32,40},{40,48},{48,56},{56,64},{64,7... | collective-permute-start | bytes 1769480 | tf_op jit(solution)/shard_map/while/body/eval_jaxpr/ppermute | solution.py:13
  377.2 16.4 %collective-permute-start = (bf16[128,1152]{1,0:T(8,128)(2,1)S(1)}, bf16[128,1152]{1,0:T(8,128)(2,1)}, u32[]{:S(2)}, u32[]{:S(2)}) collective-permute-start(bf16[128,1152]{1,0:T(8,128)(2,1)S(1)} %copy.11), channel_id=1, source_target_pairs={{0,8},{8,16},{16,24},{24,32},{32,40},{40,48},{48,56},{56,64},{64,7... | collective-permute-start | bytes 884744 | tf_op jit(solution)/shard_map/while/body/eval_jaxpr/ppermute | solution.py:13
  397.9 16.4 %collective-permute-start.1 = (f32[128,1152]{1,0:T(8,128)}, f32[128,1152]{1,0:T(8,128)S(1)}, u32[]{:S(2)}, u32[]{:S(2)}) collective-permute-start(f32[128,1152]{1,0:T(8,128)} %convolution_add_fusion.4), channel_id=1, source_target_pairs={{0,8},{8,16},{16,24},{24,32},{32,40},{40,48},{48,56},{56,64},{64,7... | collective-permute-start | bytes 1769480 | tf_op jit(solution)/shard_map/while/body/eval_jaxpr/ppermute | solution.py:13
  397.9 16.4 %collective-permute-start = (bf16[128,1152]{1,0:T(8,128)(2,1)S(1)}, bf16[128,1152]{1,0:T(8,128)(2,1)}, u32[]{:S(2)}, u32[]{:S(2)}) collective-permute-start(bf16[128,1152]{1,0:T(8,128)(2,1)S(1)} %copy.11), channel_id=1, source_target_pairs={{0,8},{8,16},{16,24},{24,32},{32,40},{40,48},{48,56},{56,64},{64,7... | collective-permute-start | bytes 884744 | tf_op jit(solution)/shard_map/while/body/eval_jaxpr/ppermute | solution.py:13
  418.6 16.4 %collective-permute-start.1 = (f32[128,1152]{1,0:T(8,128)}, f32[128,1152]{1,0:T(8,128)S(1)}, u32[]{:S(2)}, u32[]{:S(2)}) collective-permute-start(f32[128,1152]{1,0:T(8,128)} %convolution_add_fusion.4), channel_id=1, source_target_pairs={{0,8},{8,16},{16,24},{24,32},{32,40},{40,48},{48,56},{56,64},{64,7... | collective-permute-start | bytes 1769480 | tf_op jit(solution)/shard_map/while/body/eval_jaxpr/ppermute | solution.py:13
  418.6 16.4 %collective-permute-start = (bf16[128,1152]{1,0:T(8,128)(2,1)S(1)}, bf16[128,1152]{1,0:T(8,128)(2,1)}, u32[]{:S(2)}, u32[]{:S(2)}) collective-permute-start(bf16[128,1152]{1,0:T(8,128)(2,1)S(1)} %copy.11), channel_id=1, source_target_pairs={{0,8},{8,16},{16,24},{24,32},{32,40},{40,48},{48,56},{56,64},{64,7... | collective-permute-start | bytes 884744 | tf_op jit(solution)/shard_map/while/body/eval_jaxpr/ppermute | solution.py:13
  439.4 16.4 %collective-permute-start.1 = (f32[128,1152]{1,0:T(8,128)}, f32[128,1152]{1,0:T(8,128)S(1)}, u32[]{:S(2)}, u32[]{:S(2)}) collective-permute-start(f32[128,1152]{1,0:T(8,128)} %convolution_add_fusion.4), channel_id=1, source_target_pairs={{0,8},{8,16},{16,24},{24,32},{32,40},{40,48},{48,56},{56,64},{64,7... | collective-permute-start | bytes 1769480 | tf_op jit(solution)/shard_map/while/body/eval_jaxpr/ppermute | solution.py:13
  439.4 16.4 %collective-permute-start = (bf16[128,1152]{1,0:T(8,128)(2,1)S(1)}, bf16[128,1152]{1,0:T(8,128)(2,1)}, u32[]{:S(2)}, u32[]{:S(2)}) collective-permute-start(bf16[128,1152]{1,0:T(8,128)(2,1)S(1)} %copy.11), channel_id=1, source_target_pairs={{0,8},{8,16},{16,24},{24,32},{32,40},{40,48},{48,56},{56,64},{64,7... | collective-permute-start | bytes 884744 | tf_op jit(solution)/shard_map/while/body/eval_jaxpr/ppermute | solution.py:13
  460.1 16.4 %collective-permute-start.1 = (f32[128,1152]{1,0:T(8,128)}, f32[128,1152]{1,0:T(8,128)S(1)}, u32[]{:S(2)}, u32[]{:S(2)}) collective-permute-start(f32[128,1152]{1,0:T(8,128)} %convolution_add_fusion.4), channel_id=1, source_target_pairs={{0,8},{8,16},{16,24},{24,32},{32,40},{40,48},{48,56},{56,64},{64,7... | collective-permute-start | bytes 1769480 | tf_op jit(solution)/shard_map/while/body/eval_jaxpr/ppermute | solution.py:13
  460.1 16.4 %collective-permute-start = (bf16[128,1152]{1,0:T(8,128)(2,1)S(1)}, bf16[128,1152]{1,0:T(8,128)(2,1)}, u32[]{:S(2)}, u32[]{:S(2)}) collective-permute-start(bf16[128,1152]{1,0:T(8,128)(2,1)S(1)} %copy.11), channel_id=1, source_target_pairs={{0,8},{8,16},{16,24},{24,32},{32,40},{40,48},{48,56},{56,64},{64,7... | collective-permute-start | bytes 884744 | tf_op jit(solution)/shard_map/while/body/eval_jaxpr/ppermute | solution.py:13
  (14 other events, 157.0 us)
Sparse Core Ops, SparseCore 0:
  9.6 57.8 all-gather.2
  69.1 72.6 all-gather.4
  481.4 67.4 reduce-scatter.1
